TPU v7x, 128 devices: a whole 4x4x4 slice. The times are simulated.
128 devices in a mesh: grp: 8 (over z_hi, x), ep: 8 (over y, core), tp: 2 (over z_lo).
Axes of the slice: x: 4, y: 4, z: 4 (z_hi: 2, z_lo: 2; z = z_hi * 2 + z_lo), core: 2. Of those that a mesh axis runs over, the one named last changes fastest.
Arguments:
- residual: bfloat16 [2048, 4096], P(('grp', 'ep'), 'tp'), may hold values from -400 to 400
- queries: bfloat16 [2048, 4096], P(('grp', 'ep'), 'tp'), may hold values from -8 to 8
- token_key_value: bfloat16 [2048, 2, 1024], P(('grp', 'ep'), None, 'tp'), may hold values from -4 to 4
- cache: bfloat16 [2048, 2, 192, 1024], P(('grp', 'ep'), None, None, 'tp'), may hold values from -8 to 8
- cache_length: int32 [2048], P(('grp', 'ep')), may hold values from 2 to 192, as said below
- active: int32 [2048], P(('grp', 'ep')), may hold values from 0 to 1, as said below
- routes: int32 [2048, 2], P(('grp', 'ep')), may hold values from 0 to 7, as said below
- norm_gain: bfloat16 [4096], P('tp'), may hold values from 0.099609375 to 1.8984375
- router: bfloat16 [4096, 8], P('tp'), may hold values from -0.09375 to 0.09375
- w_gate: bfloat16 [8, 4096, 8192], P('ep', ('grp', 'tp')), may hold values from -0.09375 to 0.09375
- w_up: bfloat16 [8, 4096, 8192], P('ep', ('grp', 'tp')), may hold values from -0.09375 to 0.09375
- w_down: bfloat16 [8, 4096, 8192], P('ep', ('grp', 'tp')), may hold values from -0.0625 to 0.0625
Outputs:
- delta: bfloat16 [2048, 4096], P(('grp', 'ep'), 'tp')
Inputs may be any that keep to these rules, and one draw needn't show every extreme that they name: `cache_length`: every device's 32 sequences include one with 192 cached positions. The sequences that name their group's common expert first (see routes) all have active = 1. `routes`: each sequence names two different experts; among the sequences of one device no expert is named more than 16 times, and one expert, the same for every device of a grp index, is named first by exactly 16 of each such device's sequences.
All inputs are finite; a program needn't handle non-finite values.
Results may differ from a plain program's by a relative error of at most 0.012.
Values may be sent and summed in bfloat16 or wider, within the bound.
A program may use at most 192 MiB of HBM per device.

v0:
```python
import jax
import jax.numpy as jnp
from jax import lax
from jax.sharding import PartitionSpec as P

MODEL_WIDTH = 4096
QUERY_HEADS = 32
KEY_VALUE_HEADS = 8
HEAD_SIZE = 128


EPSILON = 1e-05


def attend_local(queries, token_key_value, cache, cache_length):
    seq_count = queries.shape[0]
    positions = cache.shape[2]
    heads_kv = cache.shape[3] // HEAD_SIZE
    group_share = QUERY_HEADS // KEY_VALUE_HEADS
    score_scale = HEAD_SIZE ** (-0.5)
    query_head_rows = queries.reshape(seq_count, heads_kv, group_share, HEAD_SIZE)
    stored_keys = cache[:, 0].reshape(seq_count, positions, heads_kv, HEAD_SIZE)
    stored_values = cache[:, 1].reshape(seq_count, positions, heads_kv, HEAD_SIZE)
    incoming_key = token_key_value[:, 0].reshape(seq_count, heads_kv, HEAD_SIZE)
    incoming_value = token_key_value[:, 1].reshape(seq_count, heads_kv, HEAD_SIZE)
    scores = (
        jnp.einsum(
            "skgd,slkd->skgl", query_head_rows, stored_keys, preferred_element_type=jnp.float32
        )
        * score_scale
    )
    in_cache = (
        jnp.arange(positions, dtype=jnp.int32)[None, None, None, :]
        < cache_length[:, None, None, None]
    )
    scores = jnp.where(in_cache, scores, -jnp.inf)
    self_score = (
        jnp.einsum(
            "skgd,skd->skg", query_head_rows, incoming_key, preferred_element_type=jnp.float32
        )
        * score_scale
    )
    highest = jnp.maximum(jnp.max(scores, axis=-1), self_score)
    exponent = jnp.exp(scores - highest[..., None])
    own_exp = jnp.exp(self_score - highest)
    totals = jnp.sum(exponent, axis=-1) + own_exp
    normalized = (exponent / totals[..., None]).astype(jnp.bfloat16)
    own_weight = (own_exp / totals).astype(jnp.bfloat16)
    mixture = jnp.einsum(
        "skgl,slkd->skgd", normalized, stored_values, preferred_element_type=jnp.float32
    )
    mixture = (
        mixture
        + own_weight.astype(jnp.float32)[..., None]
        * incoming_value.astype(jnp.float32)[:, :, None, :]
    )
    return mixture.reshape(seq_count, heads_kv * group_share * HEAD_SIZE).astype(jnp.bfloat16)


def per_device(
    residual,
    queries,
    token_key_value,
    cache,
    cache_length,
    active,
    routes,
    norm_gain,
    router,
    w_gate,
    w_up,
    w_down,
):
    tp_count = lax.axis_size("tp")
    tp_rank = lax.axis_index("tp")
    gate_serve, up_serve = (
        lax.all_to_all(w_gate, ("grp", "tp"), split_axis=2, concat_axis=1, tiled=True),
        lax.all_to_all(w_up, ("grp", "tp"), split_axis=2, concat_axis=1, tiled=True),
    )
    attention_output = attend_local(queries, token_key_value, cache, cache_length)
    state = residual.astype(jnp.float32) + attention_output.astype(jnp.float32)
    scaled = state * norm_gain.astype(jnp.float32)[None, :]
    squares, raw_logits = lax.psum(
        (
            jnp.sum(state * state, axis=1),
            jnp.dot(scaled, router.astype(jnp.float32), precision=lax.Precision.HIGHEST),
        ),
        "tp",
    )
    row_scale = jnp.sqrt(squares / MODEL_WIDTH + EPSILON)[:, None]
    logits = raw_logits / row_scale
    normed = lax.all_gather((scaled / row_scale).astype(jnp.bfloat16), "tp", axis=1, tiled=True)
    chosen = jnp.take_along_axis(logits, routes, axis=1)
    weight_first = jax.nn.sigmoid(chosen[:, 0] - chosen[:, 1])
    weight_second = 1.0 - weight_first
    seq_count = residual.shape[0]
    expert_count = router.shape[1]
    half_cap = seq_count // 2 // tp_count
    slot_total = half_cap * expert_count
    still_live = active == 1
    flat_expert = routes.reshape(-1)
    flat_live = jnp.repeat(still_live, 2)
    onehot = (
        (flat_expert[:, None] == jnp.arange(expert_count, dtype=jnp.int32)[None, :])
        & flat_live[:, None]
    ).astype(jnp.int32)
    before = jnp.cumsum(onehot, axis=0) - onehot
    rank_order = jnp.sum(before * onehot, axis=1)
    owner_half = rank_order // half_cap
    slot_index = rank_order % half_cap * expert_count + flat_expert
    on_this_half = flat_live & (owner_half == tp_rank)
    selector = (
        (
            (slot_index[:, None] == jnp.arange(slot_total, dtype=jnp.int32)[None, :])
            & on_this_half[:, None]
        )
        .astype(jnp.bfloat16)
        .reshape(seq_count, 2, slot_total)
    )
    senders = selector[:, 0] + selector[:, 1]
    outgoing = lax.dot_general(
        senders, normed, (((0,), (0,)), ((), ())), preferred_element_type=jnp.float32
    )
    outgoing = outgoing.astype(jnp.bfloat16).reshape(half_cap, expert_count, normed.shape[1])
    arrived = lax.all_to_all(outgoing, "ep", split_axis=1, concat_axis=0, tiled=True)
    portion = lax.all_gather(arrived, ("grp", "tp"), axis=0, tiled=True)
    gate_part = jnp.einsum("red,edf->ref", portion, gate_serve, preferred_element_type=jnp.float32)
    up_part = jnp.einsum("red,edf->ref", portion, up_serve, preferred_element_type=jnp.float32)
    hidden = (jax.nn.silu(gate_part) * up_part).astype(jnp.bfloat16)
    partial_sums = jnp.einsum(
        "ref,edf->red",
        lax.all_gather(hidden, ("grp", "tp"), axis=2, tiled=True),
        w_down,
        preferred_element_type=jnp.float32,
    )
    results = lax.all_to_all(
        partial_sums.astype(jnp.bfloat16), ("grp", "tp"), split_axis=0, concat_axis=2, tiled=True
    )
    returned = lax.all_to_all(results, "ep", split_axis=0, concat_axis=1, tiled=True).reshape(
        slot_total, normed.shape[1]
    )
    pick_first = jnp.dot(selector[:, 0], returned, preferred_element_type=jnp.float32)
    pick_second = jnp.dot(selector[:, 1], returned, preferred_element_type=jnp.float32)
    combined = weight_first[:, None] * pick_first + weight_second[:, None] * pick_second
    moe_sum = lax.psum_scatter(
        combined.astype(jnp.bfloat16), "tp", scatter_dimension=1, tiled=True
    ).astype(jnp.float32)
    delta = jnp.where(still_live[:, None], attention_output.astype(jnp.float32) + moe_sum, 0.0)
    return delta.astype(jnp.bfloat16)


def solution(mesh):
    in_specs = (
        P(("grp", "ep"), "tp"),
        P(("grp", "ep"), "tp"),
        P(("grp", "ep"), None, "tp"),
        P(("grp", "ep"), None, None, "tp"),
        P(("grp", "ep")),
        P(("grp", "ep")),
        P(("grp", "ep"), None),
        P("tp"),
        P("tp", None),
        P("ep", ("grp", "tp"), None),
        P("ep", ("grp", "tp"), None),
        P("ep", ("grp", "tp"), None),
    )
    out_specs = P(("grp", "ep"), "tp")
    return jax.shard_map(
        per_device, mesh=mesh, in_specs=in_specs, out_specs=out_specs, check_vma=False
    )
```

profile of v0, /device:TPU:1, one launch (start us, length us, event | category | flops | bytes accessed | tf_op | source)
XLA Modules:
  0.0 794.2 jit_solution(5515043613989613150)
XLA Ops:
  6.5 10.5 %fusion.74 = (bf16[32,1,192,512]{3,2,1,0:T(8,128)(2,1)}, bf16[32,1,192,512]{3,2,1,0:T(8,128)(2,1)}) fusion(bf16[32,2,192,512]{3,2,1,0:T(8,128)(2,1)} %param.15), kind=kLoop, calls=%fused_computation.95 | loop fusion | bytes 25165824 | tf_op jit(solution)/shard_map/slice | solution.py:22
  17.1 9.8 %reshape_squeeze.10 = bf16[32,192,4,128]{3,2,1,0:T(4,128)(2,1)} reshape(bf16[32,1,192,512]{3,2,1,0:T(8,128)(2,1)} %get-tuple-element.9) | data formatting | bytes 12582912 | tf_op jit(solution)/shard_map/reshape;squeeze | solution.py:22
  27.4 6.2 fusion.75
  33.7 0.5 fusion.49
  34.2 9.8 %reshape_squeeze.12 = bf16[32,192,4,128]{3,2,1,0:T(4,128)(2,1)} reshape(bf16[32,1,192,512]{3,2,1,0:T(8,128)(2,1)} %get-tuple-element.10) | data formatting | bytes 12582912 | tf_op jit(solution)/shard_map/reshape;squeeze | solution.py:23
  44.0 4.6 fusion.39
  49.1 4.9 all-reduce
  55.1 4.5 all_gather.9
  59.9 0.3 fusion.10
  60.5 16.5 %all_to_all.82 = bf16[8,8,4096]{2,0,1:T(8,128)(2,1)} all-to-all(bf16[8,8,4096]{2,0,1:T(8,128)(2,1)S(1)} %copy.90), channel_id=1, replica_groups=mesh['grp'=8,'ep'=8,'tp'=2] {'ep'}, dimensions={1} | all-to-all | bytes 1048576 | tf_op jit(solution)/shard_map/all_to_all | solution.py:125
  77.0 18.0 %copy.91 = bf16[1,256,8192]{1,0,2:T(2,128)(2,1)} copy(bf16[1,256,8192]{2,1,0:T(8,128)(2,1)} %param.21) | data formatting | bytes 8388608 | tf_op args[9]
  94.9 0.5 broadcast.143
  95.5 43.5 %reduce.4 = bf16[8192,256]{1,0:T(8,128)(2,1)} reduce(bf16[8192,1,256]{2,1,0:T(2,128)(2,1)} %bitcast.117, bf16[]{:T(256)} %broadcast.143), dimensions={1}, to_apply=%bitcast.106.reduce_sub_computation | reduce | bytes 8388610
  138.9 10.5 %reshape.180 = bf16[16,2,65536]{2,1,0:T(2,128)(2,1)} reshape(bf16[8192,256]{1,0:T(8,128)(2,1)} %reduce.4) | data formatting | bytes 8388608
  149.4 7.7 all-to-all-start.1
  157.1 17.9 %copy.93 = bf16[1,256,8192]{1,0,2:T(2,128)(2,1)} copy(bf16[1,256,8192]{2,1,0:T(8,128)(2,1)} %param.22) | data formatting | bytes 8388608 | tf_op args[10]
  175.0 43.5 %reduce.5 = bf16[8192,256]{1,0:T(8,128)(2,1)} reduce(bf16[8192,1,256]{2,1,0:T(2,128)(2,1)} %bitcast.120, bf16[]{:T(256)} %broadcast.143), dimensions={1}, to_apply=%bitcast.108.reduce_sub_computation | reduce | bytes 8388610
  218.5 10.5 %reshape.182 = bf16[16,2,65536]{2,1,0:T(2,128)(2,1)} reshape(bf16[8192,256]{1,0:T(8,128)(2,1)} %reduce.5) | data formatting | bytes 8388608
  229.0 8.5 %all-to-all-done.1 = bf16[16,2,65536]{2,1,0:T(2,128)(2,1)} async-done(((bf16[16,2,65536]{2,1,0:T(2,128)(2,1)}), bf16[16,2,65536]{2,1,0:T(2,128)(2,1)}, u32[]{:S(2)}, u32[]{:S(2)}) %all-to-all-start.1) | async-done | bytes 4194336 | tf_op jit(solution)/shard_map/all_to_all | solution.py:77
  237.5 10.9 %all-to-all-start.2 = ((bf16[16,2,65536]{2,1,0:T(2,128)(2,1)}), bf16[16,2,65536]{2,1,0:T(2,128)(2,1)}, u32[]{:S(2)}, u32[]{:S(2)}) async-start(bf16[16,2,65536]{2,1,0:T(2,128)(2,1)} %reshape.182), calls=%async_computation.2 | async-start | bytes 8388608 | tf_op jit(solution)/shard_map/all_to_all | solution.py:78
  248.5 12.4 %reshape.181 = bf16[8192,1,256]{2,1,0:T(2,128)(2,1)} reshape(bf16[16,2,65536]{2,1,0:T(2,128)(2,1)} %all-to-all-done.1) | data formatting | bytes 8388608
  260.9 6.1 copy.101
  266.9 6.4 copy.92
  273.3 50.0 %all-to-all-done.2 = bf16[16,2,65536]{2,1,0:T(2,128)(2,1)} async-done(((bf16[16,2,65536]{2,1,0:T(2,128)(2,1)}), bf16[16,2,65536]{2,1,0:T(2,128)(2,1)}, u32[]{:S(2)}, u32[]{:S(2)}) %all-to-all-start.2) | async-done | bytes 4194336 | tf_op jit(solution)/shard_map/all_to_all | solution.py:78
  323.3 12.4 %reshape.183 = bf16[8192,1,256]{2,1,0:T(2,128)(2,1)} reshape(bf16[16,2,65536]{2,1,0:T(2,128)(2,1)} %all-to-all-done.2) | data formatting | bytes 8388608
  335.7 6.1 copy.102
  341.8 6.4 copy.94
  348.2 5.4 all-gather.3.cloned.1.call-done
  353.7 8.5 %fusion.4 = f32[1024,512]{1,0:T(8,128)S(1)} fusion(bf16[4096,512]{1,0:T(8,128)(2,1)} %bitcast.125, bf16[1024,1,4096]{2,0,1:T(8,128)(2,1)} %all-gather.3.cloned.1.call-done), kind=kOutput, calls=%fused_computation.5 | convolution fusion | flops 4294967296 | bytes 14680064 | tf_op jit(solution)/shard_map/red,edf->ref/dot_general | solution.py:127
  362.2 5.7 fusion.14
  367.9 347.5 %all-gather.5.cloned.1.call-done = bf16[1024,1,8192]{2,0,1:T(8,128)(2,1)} async-done(((bf16[1024,1,512]{2,0,1:T(8,128)(2,1)}), bf16[1024,1,8192]{2,0,1:T(8,128)(2,1)}) %all-gather.5.cloned.1.call-update) | async-done | bytes 16777232 | tf_op jit(solution)/shard_map/all_gather | solution.py:132
  715.5 11.5 %fusion.25 = bf16[1024,1,256]{2,0,1:T(8,128)(2,1)S(1)} fusion(bf16[1,256,8192]{2,1,0:T(8,128)(2,1)} %param.23, bf16[1024,1,8192]{2,0,1:T(8,128)(2,1)} %all-gather.5.cloned.1.call-done), kind=kOutput, calls=%fused_computation.26 | convolution fusion | flops 4295229440 | bytes 21495808 | tf_op jit(solution)/shard_map/ref,edf->red/dot_general | solution.py:130
  727.0 1.0 reduce.6
  728.0 0.9 reshape.184
  728.9 11.3 %all-to-all-start.3 = ((bf16[16,2,8192]{2,1,0:T(2,128)(2,1)}), bf16[16,2,8192]{2,1,0:T(2,128)(2,1)S(1)}, u32[]{:S(2)}, u32[]{:S(2)}) async-start(bf16[16,2,8192]{2,1,0:T(2,128)(2,1)} %reshape.184), calls=%async_computation.3 | async-start | bytes 1048576 | tf_op jit(solution)/shard_map/all_to_all | solution.py:136
  740.8 10.2 %all-to-all-done.3 = bf16[16,2,8192]{2,1,0:T(2,128)(2,1)S(1)} async-done(((bf16[16,2,8192]{2,1,0:T(2,128)(2,1)}), bf16[16,2,8192]{2,1,0:T(2,128)(2,1)S(1)}, u32[]{:S(2)}, u32[]{:S(2)}) %all-to-all-start.3) | async-done | bytes 524320 | tf_op jit(solution)/shard_map/all_to_all | solution.py:136
  750.9 0.5 reshape.185
  752.1 3.9 reduce.7
  756.1 1.3 reshape.186
  757.4 6.0 all-to-all-start.4
  763.4 0.7 gather_fusion
  764.5 8.3 %all-to-all-done.4 = bf16[8,2,16384]{2,1,0:T(2,128)(2,1)S(1)} async-done(((bf16[8,2,16384]{2,1,0:T(2,128)(2,1)}), bf16[8,2,16384]{2,1,0:T(2,128)(2,1)S(1)}, u32[]{:S(2)}, u32[]{:S(2)}) %all-to-all-start.4) | async-done | bytes 524320 | tf_op jit(solution)/shard_map/all_to_all | solution.py:139
  772.8 0.5 reshape.187
  773.3 0.6 copy.132
  773.9 0.4 convolution_multiply_fusion.1
  774.3 1.1 fusion.12
  775.5 10.6 %reduce-scatter.2.cloned.1.call-done = bf16[32,2048]{1,0:T(8,128)(2,1)} async-done(((bf16[32,4096]{1,0:T(8,128)(2,1)}), bf16[32,2048]{1,0:T(8,128)(2,1)}) %reduce-scatter.2.cloned.1.call-update) | async-done | bytes 131088 | tf_op jit(solution)/shard_map/reduce_scatter | solution.py:145
  786.1 1.6 select_convert_fusion
  (71 shorter events, 4.2 us)
Async XLA Ops:
  6.5 42.4 %copy-start = (bf16[2048,8]{0,1:T(8,128)(2,1)S(1)}, bf16[2048,8]{0,1:T(8,128)(2,1)}, u32[]{:S(2)}) copy-start(bf16[2048,8]{0,1:T(8,128)(2,1)} %param.20) | copy-start | bytes 98308
  6.5 347.1 %all-gather.3.cloned.1.call-start = ((), (), s32[]{:S(2)}) async-start(), calls=%async_computation.6 | async-start | bytes 8912896 | tf_op jit(solution)/shard_map/all_gather | solution.py:126
  17.1 9.8 %copy-start.4 = (bf16[32,2048]{1,0:T(8,128)(2,1)S(1)}, bf16[32,2048]{1,0:T(8,128)(2,1)}, u32[]{:S(2)}) copy-start(bf16[32,2048]{1,0:T(8,128)(2,1)} %param.13) | copy-start | bytes 393220
  17.1 9.9 %copy-start.8 = (s32[32]{0:T(128)S(1)}, s32[32]{0:T(128)}, u32[]{:S(2)}) copy-start(s32[32]{0:T(128)} %param.16) | copy-start | bytes 388
  17.1 10.0 %copy-start.5 = (bf16[32,2,512]{2,1,0:T(2,128)(2,1)S(1)}, bf16[32,2,512]{2,1,0:T(2,128)(2,1)}, u32[]{:S(2)}) copy-start(bf16[32,2,512]{2,1,0:T(2,128)(2,1)} %param.14) | copy-start | bytes 196612
  44.0 4.8 copy-start.6
  44.0 4.8 copy-start.3
  44.0 10.0 %copy-start.7 = (s32[32,2]{0,1:T(2,128)S(1)}, s32[32,2]{0,1:T(2,128)}, u32[]{:S(2)}) copy-start(s32[32,2]{0,1:T(2,128)} %param.18) | copy-start | bytes 772
  44.0 10.2 %copy-start.10 = (s32[32]{0:T(128)S(1)}, s32[32]{0:T(128)}, u32[]{:S(2)}) copy-start(s32[32]{0:T(128)} %param.17) | copy-start | bytes 388
  149.4 88.1 %all-to-all-start.1 = ((bf16[16,2,65536]{2,1,0:T(2,128)(2,1)}), bf16[16,2,65536]{2,1,0:T(2,128)(2,1)}, u32[]{:S(2)}, u32[]{:S(2)}) async-start(bf16[16,2,65536]{2,1,0:T(2,128)(2,1)} %reshape.180), calls=%async_computation.1 | async-start | bytes 8388608 | tf_op jit(solution)/shard_map/all_to_all | solution.py:77
  237.5 85.8 %all-to-all-start.2 = ((bf16[16,2,65536]{2,1,0:T(2,128)(2,1)}), bf16[16,2,65536]{2,1,0:T(2,128)(2,1)}, u32[]{:S(2)}, u32[]{:S(2)}) async-start(bf16[16,2,65536]{2,1,0:T(2,128)(2,1)} %reshape.182), calls=%async_computation.2 | async-start | bytes 8388608 | tf_op jit(solution)/shard_map/all_to_all | solution.py:78
  248.4 467.1 %all-gather.5.cloned.1.call-start = ((), (), s32[]{:S(2)}) async-start(), calls=%async_computation.7 | async-start | bytes 17825792 | tf_op jit(solution)/shard_map/all_gather | solution.py:132
  353.7 8.5 %copy-start.2 = (bf16[1,16,256,512]{3,2,1,0:T(8,128)(2,1)S(1)}, bf16[1,16,256,512]{3,2,1,0:T(8,128)(2,1)}, u32[]{:S(2)}) copy-start(bf16[1,16,256,512]{3,2,1,0:T(8,128)(2,1)} %copy.94) | copy-start | bytes 12582916
  353.7 8.5 %copy-start.9 = (bf16[1024,1,4096]{2,0,1:T(8,128)(2,1)S(1)}, bf16[1024,1,4096]{2,0,1:T(8,128)(2,1)}, u32[]{:S(2)}) copy-start(bf16[1024,1,4096]{2,0,1:T(8,128)(2,1)} %all-gather.3.cloned.1.call-done) | copy-start | bytes 25165828
  728.9 22.0 %all-to-all-start.3 = ((bf16[16,2,8192]{2,1,0:T(2,128)(2,1)}), bf16[16,2,8192]{2,1,0:T(2,128)(2,1)S(1)}, u32[]{:S(2)}, u32[]{:S(2)}) async-start(bf16[16,2,8192]{2,1,0:T(2,128)(2,1)} %reshape.184), calls=%async_computation.3 | async-start | bytes 1048576 | tf_op jit(solution)/shard_map/all_to_all | solution.py:136
  757.4 15.4 %all-to-all-start.4 = ((bf16[8,2,16384]{2,1,0:T(2,128)(2,1)}), bf16[8,2,16384]{2,1,0:T(2,128)(2,1)S(1)}, u32[]{:S(2)}, u32[]{:S(2)}) async-start(bf16[8,2,16384]{2,1,0:T(2,128)(2,1)} %reshape.186), calls=%async_computation.4 | async-start | bytes 1048576 | tf_op jit(solution)/shard_map/all_to_all | solution.py:139
  763.4 22.6 %reduce-scatter.2.cloned.1.call-start = ((), (), s32[]{:S(2)}) async-start(), calls=%async_computation.8 | async-start | bytes 393216 | tf_op jit(solution)/shard_map/reduce_scatter | solution.py:145
  763.4 24.3 %copy-start.1 = (bf16[2048,8]{0,1:T(8,128)(2,1)S(1)}, bf16[2048,8]{0,1:T(8,128)(2,1)}, u32[]{:S(2)}) copy-start(bf16[2048,8]{0,1:T(8,128)(2,1)} %param.20) | copy-start | bytes 98308
Sparse Core Ops, SparseCore 0:
  77.1 276.5 all-gather.2
  368.1 347.3 all-gather.4
  775.6 10.3 reduce-scatter.1
where the time goes:
time: 797 us; the launch traced here: 794 us
  waiting for transfers between devices  441 us (55%)
  local copies, waits for them, and re-layouts  144 us (18%)
  other arithmetic  95.3 us (12%)
  matrix products  39 us (5%)
  starting transfers between devices  36 us (5%)
  blocking collectives  25.8 us (3%)
  between operations  13.4 us (2%)
    all_gather x1, waiting for transfers between devices, per_device(): lax.all_gather(hidden, ('grp', 'tp'), axis=2, tiled=True)  348 us
    unnamed x38, local copies, waits for them, and re-layouts  98.4 us
    unnamed x2, other arithmetic  86.9 us
    all_to_all x1, waiting for transfers between devices, per_device(): lax.all_to_all(w_up, ('grp', 'tp'), split_axis=2, concat_axis=1, tiled=True)  50 us
    all_to_all x1, blocking collectives, per_device(): lax.all_to_all(outgoing, 'ep', split_axis=1, concat_axis=0, tiled=True)  16.5 us
  transfers between devices with their start and end apart: 7, of which 7 were waited for; matrix products, arithmetic and copies ran while one was open for 25% of the time, Pallas kernels for 0%

commit v1 on v0

--- a/solution.py
+++ b/solution.py
@@ -1,6 +1,8 @@
 import jax
 import jax.numpy as jnp
 from jax import lax
+from jax.experimental import pallas as pl
+from jax.experimental.pallas import tpu as pltpu
 from jax.sharding import PartitionSpec as P
 
 MODEL_WIDTH = 4096
@@ -10,6 +12,295 @@
 
 
 EPSILON = 1e-05
+
+SIDE = 4
+ROWS = 64
+DBLK = 256
+DSET = SIDE * DBLK
+FBLK = 2048
+FT = 512
+MESH_AXES = ("grp", "ep", "tp")
+MESH_ID = pl.DeviceIdType.MESH
+
+
+def line_permutation(step):
+    pairs = []
+    for grp in range(8):
+        for ep in range(8):
+            for tp in range(2):
+                x, z = grp % 4, (grp // 4) * 2 + tp
+                if ep % 2 == 0:
+                    x2, z2 = (x + step) % SIDE, z
+                else:
+                    x2, z2 = x, (z + step) % SIDE
+                pairs.append(((grp * 8 + ep) * 2 + tp, (((z2 // 2) * 4 + x2) * 8 + ep) * 2 + z2 % 2))
+    return pairs
+
+
+def coordinates():
+    grp, ep, tp = (lax.axis_index(name) for name in MESH_AXES)
+    x = lax.rem(grp, 4)
+    z = lax.div(grp, 4) * 2 + tp
+    core = lax.rem(ep, 2)
+    return x + (z - x) * core, z + (x - z) * core, core, ep
+
+
+def moe_kernel(
+    x_in, w_gate, w_up, w_down, g1, g2, g3, u1, u2, u3, d1, d2, d3, y_out,
+    rows, wg, wu, wd, send, fwd, got, own, hid, part, part32, part_in, y_send,
+    w_sem, xs_send, xs_recv, x_local, xa_send, xa_recv, rs_send, rs_recv, ag_send, ag_recv,
+    o_send, o_recv, y_ssem, y_rsem, y_local,
+):
+    a, b, core, ep = coordinates()
+
+    def place(at_a, at_b):
+        return at_a + (at_b - at_a) * core, at_b + (at_a - at_b) * core
+
+    def peer(at_a, at_b):
+        x, z = place(at_a, at_b)
+        return (lax.div(z, 2) * 4 + x, ep, lax.rem(z, 2))
+
+    def block(at_a, at_b):
+        x, z = place(at_a, at_b)
+        return pl.multiple_of((lax.div(z, 2) * 8 + x * 2 + lax.rem(z, 2)) * DBLK, DBLK)
+
+    def shifted(value, by):
+        return lax.rem(value + by + SIDE, SIDE)
+
+    def remote(src, dst, ssem, rsem, to):
+        return pltpu.make_async_remote_copy(
+            src_ref=src, dst_ref=dst, send_sem=ssem, recv_sem=rsem, device_id=to, device_id_type=MESH_ID
+        )
+
+    right, left, across = shifted(b, 1), shifted(b, -1), shifted(b, 2)
+
+    loads = []
+    for which, (full, parts, dst) in enumerate(
+        ((w_gate, (g1, g2, g3), wg), (w_up, (u1, u2, u3), wu), (w_down, (d1, d2, d3), wd))
+    ):
+        column = pl.ds(pl.multiple_of(a * FBLK, FBLK), FBLK)
+        for step in range(SIDE):
+            row = pl.ds(pl.multiple_of(shifted(a, -step) * DBLK, DBLK), DBLK)
+            src = full.at[:, column] if step == 0 else parts[step - 1]
+            copy = pltpu.make_async_copy(src, dst.at[row], w_sem.at[which, step])
+            copy.start()
+            loads.append(copy)
+
+    barrier = pltpu.get_barrier_semaphore()
+    for step in range(1, SIDE):
+        pl.semaphore_signal(barrier, inc=1, device_id=peer(shifted(a, step), b), device_id_type=MESH_ID)
+        pl.semaphore_signal(barrier, inc=1, device_id=peer(a, shifted(b, step)), device_id_type=MESH_ID)
+    pl.semaphore_wait(barrier, 2 * (SIDE - 1))
+
+    copies = []
+    for step in (2, 1, 3):
+        to_b = shifted(b, step)
+        for k in range(SIDE):
+            copy = remote(
+                x_in.at[:, pl.ds(block(k, to_b), DBLK)],
+                rows.at[a, b, :, pl.ds(k * DBLK, DBLK)],
+                xs_send.at[step - 1, k], xs_recv.at[step - 1, k], peer(a, to_b),
+            )
+            copy.start()
+            copies.append(copy)
+    local = []
+    for k in range(SIDE):
+        copy = pltpu.make_async_copy(
+            x_in.at[:, pl.ds(block(k, b), DBLK)], rows.at[a, b, :, pl.ds(k * DBLK, DBLK)], x_local.at[k]
+        )
+        copy.start()
+        local.append(copy)
+    for copy in local + copies:
+        copy.wait()
+
+    copies = []
+    for step in (2, 1, 3):
+        copy = remote(
+            rows.at[a], rows.at[a], xa_send.at[step - 1], xa_recv.at[step - 1], peer(shifted(a, step), b)
+        )
+        copy.start()
+        copies.append(copy)
+    for copy in loads[: 2 * SIDE]:
+        copy.wait()
+    for copy in copies:
+        copy.wait()
+
+    def partial(group, half, tile):
+        lhs = rows[pl.ds(2 * half, 2), group].reshape(2 * ROWS, DSET)
+        cols = pl.ds(pl.multiple_of(tile * FT, FT), FT)
+        ups = pl.ds(pl.multiple_of(tile * FT + FBLK, FT), FT)
+        gate = jnp.dot(lhs, wg[:, cols], preferred_element_type=jnp.float32)
+        up = jnp.dot(lhs, wu[:, cols], preferred_element_type=jnp.float32)
+        return cols, ups, gate, up
+
+    def fill(group, half, slot, extra=None):
+        @pl.loop(0, FBLK // FT)
+        def _(tile):
+            cols, ups, gate, up = partial(group, half, tile)
+            if extra is not None:
+                gate = gate + fwd[extra, :, cols].astype(jnp.float32)
+                up = up + fwd[extra, :, ups].astype(jnp.float32)
+            send[slot, :, cols] = gate.astype(jnp.bfloat16)
+            send[slot, :, ups] = up.astype(jnp.bfloat16)
+
+    to_right, to_left = peer(a, right), peer(a, left)
+    fill(across, 0, 0)
+    over_right = remote(send.at[0], fwd.at[0], rs_send.at[0], rs_recv.at[0], to_right)
+    over_right.start()
+    fill(across, 1, 1)
+    over_left = remote(send.at[1], fwd.at[1], rs_send.at[1], rs_recv.at[1], to_left)
+    over_left.start()
+    fill(right, 1, 2)
+    plain_right = remote(send.at[2], got.at[1], rs_send.at[2], rs_recv.at[2], to_right)
+    plain_right.start()
+    fill(left, 0, 3)
+    plain_left = remote(send.at[3], got.at[2], rs_send.at[3], rs_recv.at[3], to_left)
+    plain_left.start()
+    over_right.wait()
+    fill(right, 0, 4, 0)
+    sum_right = remote(send.at[4], got.at[0], rs_send.at[4], rs_recv.at[4], to_right)
+    sum_right.start()
+    over_left.wait()
+    fill(left, 1, 5, 1)
+    sum_left = remote(send.at[5], got.at[3], rs_send.at[5], rs_recv.at[5], to_left)
+    sum_left.start()
+
+    for half in range(2):
+
+        @pl.loop(0, FBLK // FT)
+        def _(tile, half=half):
+            cols, ups, gate, up = partial(b, half, tile)
+            own[half, :, cols] = gate
+            own[half, :, ups] = up
+
+    for copy in (plain_right, plain_left, sum_right, sum_left):
+        copy.wait()
+
+    for half in range(2):
+
+        @pl.loop(0, FBLK // FT)
+        def _(tile, half=half):
+            cols = pl.ds(pl.multiple_of(tile * FT, FT), FT)
+            ups = pl.ds(pl.multiple_of(tile * FT + FBLK, FT), FT)
+            gate = (
+                own[half, :, cols]
+                + got[half, :, cols].astype(jnp.float32)
+                + got[2 + half, :, cols].astype(jnp.float32)
+            )
+            up = (
+                own[half, :, ups]
+                + got[half, :, ups].astype(jnp.float32)
+                + got[2 + half, :, ups].astype(jnp.float32)
+            )
+            value = gate / (1.0 + jnp.exp(-gate)) * up
+            hid[b, half, :, cols] = value.astype(jnp.bfloat16)
+
+    own_right = remote(hid.at[b], hid.at[b], ag_send.at[0], ag_recv.at[0], to_right)
+    own_left = remote(hid.at[b], hid.at[b], ag_send.at[1], ag_recv.at[1], to_left)
+    own_right.start()
+    own_left.start()
+    for copy in loads[2 * SIDE :]:
+        copy.wait()
+
+    o_copies = {}
+
+    def down(order, group):
+        lhs = hid[group].reshape(SIDE * ROWS, FBLK)
+
+        @pl.loop(0, DSET // DBLK)
+        def _(tile):
+            cols = pl.ds(pl.multiple_of(tile * DBLK, DBLK), DBLK)
+            out = lax.dot_general(
+                lhs, wd[cols, :], (((1,), (1,)), ((), ())), preferred_element_type=jnp.float32
+            ).reshape(SIDE, ROWS, DBLK)
+            part32[order, :, :, cols] = out
+            part[order, :, :, cols] = out.astype(jnp.bfloat16)
+
+        for step in (2, 1, 3):
+            to_a = shifted(a, step)
+            copy = remote(
+                part.at[order, to_a], part_in.at[order, step - 1],
+                o_send.at[order, step - 1], o_recv.at[order, step - 1], peer(to_a, b),
+            )
+            copy.start()
+            o_copies[order, step] = copy
+
+    y_copies = []
+
+    def finish(order, group):
+        total = part32[order, a]
+        for step in range(1, SIDE):
+            o_copies[order, step].wait()
+            total = total + part_in[order, step - 1].astype(jnp.float32)
+        y_send[order] = total.astype(jnp.bfloat16)
+        for k in range(SIDE):
+            src = y_send.at[order, :, pl.ds(k * DBLK, DBLK)]
+            dst = y_out.at[:, pl.ds(block(k, b), DBLK)]
+            if order == 0:
+                copy = pltpu.make_async_copy(src, dst, y_local.at[k])
+            else:
+                copy = remote(src, dst, y_ssem.at[order - 1, k], y_rsem.at[order - 1, k], peer(a, group))
+            copy.start()
+            y_copies.append(copy)
+
+    down(0, b)
+    own_right.wait()
+    on_right = remote(hid.at[left, 0], hid.at[left, 0], ag_send.at[2], ag_recv.at[2], to_right)
+    on_right.start()
+    own_left.wait()
+    on_left = remote(hid.at[right, 1], hid.at[right, 1], ag_send.at[3], ag_recv.at[3], to_left)
+    on_left.start()
+    down(1, left)
+    down(3, right)
+    finish(0, b)
+    on_right.wait()
+    on_left.wait()
+    down(2, across)
+    finish(1, left)
+    finish(3, right)
+    finish(2, across)
+    for copy in y_copies:
+        copy.wait()
+
+
+def expert_layer(x_in, w_gate, w_up, w_down, moved):
+    bf16, f32 = jnp.bfloat16, jnp.float32
+    dma = pltpu.SemaphoreType.DMA
+    scratch = [
+        pltpu.VMEM((SIDE, SIDE, ROWS, DSET), bf16),
+        pltpu.VMEM((DSET, FBLK), bf16),
+        pltpu.VMEM((DSET, FBLK), bf16),
+        pltpu.VMEM((DSET, FBLK), bf16),
+        pltpu.VMEM((6, 2 * ROWS, 2 * FBLK), bf16),
+        pltpu.VMEM((2, 2 * ROWS, 2 * FBLK), bf16),
+        pltpu.VMEM((4, 2 * ROWS, 2 * FBLK), bf16),
+        pltpu.VMEM((2, 2 * ROWS, 2 * FBLK), f32),
+        pltpu.VMEM((SIDE, 2, 2 * ROWS, FBLK), bf16),
+        pltpu.VMEM((SIDE, SIDE, ROWS, DSET), bf16),
+        pltpu.VMEM((SIDE, SIDE, ROWS, DSET), f32),
+        pltpu.VMEM((SIDE, SIDE - 1, ROWS, DSET), bf16),
+        pltpu.VMEM((SIDE, ROWS, DSET), bf16),
+        dma((3, SIDE)),
+        dma((3, SIDE)), dma((3, SIDE)), dma((SIDE,)),
+        dma((3,)), dma((3,)),
+        dma((6,)), dma((6,)),
+        dma((4,)), dma((4,)),
+        dma((SIDE, 3)), dma((SIDE, 3)),
+        dma((3, SIDE)), dma((3, SIDE)), dma((SIDE,)),
+    ]
+    anywhere = pl.BlockSpec(memory_space=pl.ANY)
+    return pl.pallas_call(
+        moe_kernel,
+        out_shape=jax.ShapeDtypeStruct((ROWS, MODEL_WIDTH), bf16),
+        in_specs=[anywhere] * 13,
+        out_specs=anywhere,
+        scratch_shapes=scratch,
+        compiler_params=pltpu.CompilerParams(
+            collective_id=0, has_side_effects=True, vmem_limit_bytes=60 * 1024 * 1024
+        ),
+        cost_estimate=pl.CostEstimate(flops=13 * 10**9, bytes_accessed=14 * 10**6, transcendentals=10**6),
+        name="expert_layer",
+    )(x_in, w_gate, w_up, w_down, *moved)
 
 
 def attend_local(queries, token_key_value, cache, cache_length):
@@ -73,10 +364,14 @@
 ):
     tp_count = lax.axis_size("tp")
     tp_rank = lax.axis_index("tp")
-    gate_serve, up_serve = (
-        lax.all_to_all(w_gate, ("grp", "tp"), split_axis=2, concat_axis=1, tiled=True),
-        lax.all_to_all(w_up, ("grp", "tp"), split_axis=2, concat_axis=1, tiled=True),
-    )
+    w_gate, w_up, w_down = w_gate[0], w_up[0], w_down[0]
+    line_rank = coordinates()[0]
+    moved = []
+    for weight in (w_gate, w_up, w_down):
+        for step in range(1, SIDE):
+            column = lax.rem(line_rank + step, SIDE) * FBLK
+            piece = lax.dynamic_slice(weight, (0, column), (DBLK, FBLK))
+            moved.append(lax.ppermute(piece, MESH_AXES, line_permutation(step)))
     attention_output = attend_local(queries, token_key_value, cache, cache_length)
     state = residual.astype(jnp.float32) + attention_output.astype(jnp.float32)
     scaled = state * norm_gain.astype(jnp.float32)[None, :]
@@ -123,19 +418,8 @@
     )
     outgoing = outgoing.astype(jnp.bfloat16).reshape(half_cap, expert_count, normed.shape[1])
     arrived = lax.all_to_all(outgoing, "ep", split_axis=1, concat_axis=0, tiled=True)
-    portion = lax.all_gather(arrived, ("grp", "tp"), axis=0, tiled=True)
-    gate_part = jnp.einsum("red,edf->ref", portion, gate_serve, preferred_element_type=jnp.float32)
-    up_part = jnp.einsum("red,edf->ref", portion, up_serve, preferred_element_type=jnp.float32)
-    hidden = (jax.nn.silu(gate_part) * up_part).astype(jnp.bfloat16)
-    partial_sums = jnp.einsum(
-        "ref,edf->red",
-        lax.all_gather(hidden, ("grp", "tp"), axis=2, tiled=True),
-        w_down,
-        preferred_element_type=jnp.float32,
-    )
-    results = lax.all_to_all(
-        partial_sums.astype(jnp.bfloat16), ("grp", "tp"), split_axis=0, concat_axis=2, tiled=True
-    )
+    results = expert_layer(arrived.reshape(ROWS, MODEL_WIDTH), w_gate, w_up, w_down, moved)
+    results = results.reshape(ROWS, 1, MODEL_WIDTH)
     returned = lax.all_to_all(results, "ep", split_axis=0, concat_axis=1, tiled=True).reshape(
         slot_total, normed.shape[1]
     )

time: 797 us -> 273 us (0.34)
  waiting for transfers between devices: 441 us -> 28.9 us
  Pallas kernels: 0 us -> 105 us
  local copies, waits for them, and re-layouts: 144 us -> 41.9 us
  other arithmetic: 95.3 us -> 5.4 us
  matrix products: 39 us -> 13.3 us
  blocking collectives: 25.8 us -> 38.3 us
  starting transfers between devices: 36 us -> 26 us
    all_gather x2 -> x0, waiting for transfers between devices: 353 us -> none  [the longest x1 348 us: per_device(): lax.all_gather(hidden, ('grp', 'tp'), axis=2, tiled=True)]
    pallas_call x0 -> x1, Pallas kernels: none -> 105 us  [expert_layer(): pl.pallas_call(moe_kernel, out_shape=jax.ShapeDtypeStruct((ROWS, MODEL_WI...]
    unnamed x38 -> x26, local copies, waits for them, and re-layouts: 98.4 us -> 3.32 us
    unnamed x2 -> x0, other arithmetic: 86.9 us -> none
    all_to_all x3 -> x1, waiting for transfers between devices: 68.7 us -> 8.85 us  [per_device(): lax.all_to_all(outgoing, 'ep', split_axis=1, concat_axis=0, tiled=True)]
    all_gather x1, blocking collectives: 4.49 us -> 33.8 us  [per_device(): lax.all_gather((scaled / row_scale).astype(jnp.bfloat16), 'tp', axis=1, t...]
    dot_general x3 -> x0, matrix products: 25.7 us -> none  [the longest x1 11.5 us: per_device(): jnp.einsum('ref,edf->red', lax.all_gather(hidden, ('grp', 'tp'), axis=2,...]
    all_to_all x3 -> x1, starting transfers between devices: 29.9 us -> 4.58 us  [per_device(): lax.all_to_all(outgoing, 'ep', split_axis=1, concat_axis=0, tiled=True)]
  transfers between devices with their start and end apart: 7 -> 12, of which waited for: 7 -> 3; matrix products, arithmetic and copies ran while one was open for 25% -> 18% of each run, Pallas kernels for 0% -> 0%
where the time goes in v1:
time: 273 us; the launch traced here: 272 us
  Pallas kernels  105 us (38%)
  local copies, waits for them, and re-layouts  41.9 us (15%)
  blocking collectives  38.3 us (14%)
  waiting for transfers between devices  28.9 us (11%)
  starting transfers between devices  26 us (10%)
  between operations  13.7 us (5%)
  matrix products  13.3 us (5%)
  other arithmetic  5.4 us (2%)
    pallas_call x1, Pallas kernels, expert_layer(): pl.pallas_call(moe_kernel, out_shape=jax.ShapeDtypeStruct((ROWS, MODEL_WI...  105 us
    all_gather x1, blocking collectives, per_device(): lax.all_gather((scaled / row_scale).astype(jnp.bfloat16), 'tp', axis=1, t...  33.8 us
    ppermute x9, starting transfers between devices, per_device(): moved.append(lax.ppermute(piece, MESH_AXES, line_permutation(step)))  13.1 us
    reduce_scatter x1, waiting for transfers between devices, per_device(): lax.psum_scatter(combined.astype(jnp.bfloat16), 'tp', scatter_dimension=1...  11.8 us
    dynamic_slice x3, local copies, waits for them, and re-layouts, per_device(): piece = lax.dynamic_slice(weight, (0, column), (DBLK, FBLK))  10.5 us
    another operation x1, local copies, waits for them, and re-layouts, attend_local(): cache[:, 1].reshape(seq_count, positions, heads_kv, HEAD_SIZE)  9.75 us
    another operation x1, local copies, waits for them, and re-layouts, attend_local(): stored_keys = cache[:, 0].reshape(seq_count, positions, heads_kv, HEAD_SIZE)  9.73 us
    all_to_all x1, waiting for transfers between devices, per_device(): lax.all_to_all(outgoing, 'ep', split_axis=1, concat_axis=0, tiled=True)  8.85 us
  transfers between devices with their start and end apart: 12, of which 3 were waited for; matrix products, arithmetic and copies ran while one was open for 18% of the time, Pallas kernels for 0%

profile of v1, /device:TPU:1, one launch (start us, length us, event | category | flops | bytes accessed | tf_op | source)
XLA Modules:
  0.0 272.1 jit_solution(10929540156566145114)
XLA Ops:
  6.5 3.8 %dynamic-slice_bitcast_fusion.6 = (bf16[256,2048]{1,0:T(8,128)(2,1)}, bf16[256,2048]{1,0:T(8,128)(2,1)}, bf16[256,2048]{1,0:T(8,128)(2,1)}) fusion(bf16[1,256,8192]{2,1,0:T(8,128)(2,1)} %param.21, s32[]{:T(128)S(6)} %select_n.58, s32[]{:T(128)S(6)} %select_n.56, s32[]{:T(128)S(6)} %select_n.57), kind=kLoop, calls=%fused_computation.22 | loop fusion | bytes 6291468 | tf_op jit(solution)/shard_map/dynamic_slice | solution.py:373
  10.4 2.5 collective-permute-start
  12.8 3.3 %collective-permute-start.1 = (bf16[256,2048]{1,0:T(8,128)(2,1)}, bf16[256,2048]{1,0:T(8,128)(2,1)}, u32[]{:S(2)}, u32[]{:S(2)}) collective-permute-start(bf16[256,2048]{1,0:T(8,128)(2,1)} %get-tuple-element.19), channel_id=1, source_target_pairs={{0,32},{1,33},{2,66},{3,67},{4,36},{5,37},{6,70},{7,71},{8,40},{9,... | collective-permute-start | bytes 3145736 | tf_op jit(solution)/shard_map/ppermute | solution.py:374
  16.1 0.7 collective-permute-start.2
  16.8 3.1 %dynamic-slice_bitcast_fusion.3 = (bf16[256,2048]{1,0:T(8,128)(2,1)S(1)}, bf16[256,2048]{1,0:T(8,128)(2,1)}, bf16[256,2048]{1,0:T(8,128)(2,1)S(1)}) fusion(bf16[1,256,8192]{2,1,0:T(8,128)(2,1)} %param.22, s32[]{:T(128)S(6)} %select_n.58, s32[]{:T(128)S(6)} %select_n.56, s32[]{:T(128)S(6)} %select_n.57), kind=kLoop, calls=%fused_computation.19 | loop fusion | bytes 6291468 | tf_op jit(solution)/shard_map/dynamic_slice | solution.py:373
  20.0 0.7 collective-permute-start.3
  20.7 0.4 collective-permute-start.4
  21.2 4.9 %fusion.51 = (bf16[32,1,192,512]{3,2,1,0:T(8,128)(2,1)}, bf16[32,1,192,512]{3,2,1,0:T(8,128)(2,1)}) fusion(bf16[32,2,192,512]{3,2,1,0:T(8,128)(2,1)S(1)} %copy-done.2), kind=kLoop, calls=%fused_computation.88 | loop fusion | bytes 25165824 | tf_op jit(solution)/shard_map/slice | solution.py:313
  26.0 9.7 %reshape_squeeze.10 = bf16[32,192,4,128]{3,2,1,0:T(4,128)(2,1)} reshape(bf16[32,1,192,512]{3,2,1,0:T(8,128)(2,1)} %get-tuple-element.9) | data formatting | bytes 12582912 | tf_op jit(solution)/shard_map/reshape;squeeze | solution.py:313
  36.0 0.3 fusion.32
  36.3 6.2 %fusion.52 = (f32[32,4,4]{2,1,0:T(4,128)S(1)}, f32[32,4,4,192]{3,2,1,0:T(4,128)S(1)}) fusion(bf16[32,4,4,128]{3,2,1,0:T(4,128)(2,1)S(1)} %reshape.147, bf16[32,192,4,128]{3,2,1,0:T(4,128)(2,1)} %reshape_squeeze.10, pred[32,192]{1,0:T(8,128)(4,1)S(1)} %iota_compare_fusion.2), kind=kOutput, calls=%fused_computation.89 | convolution fusion | flops 25460224 | bytes 6823936 | tf_op jit(solution)/shard_map/skgd,slkd->skgl/dot_general | solution.py:318
  42.6 0.5 fusion.26
  43.1 9.7 %reshape_squeeze.12 = bf16[32,192,4,128]{3,2,1,0:T(4,128)(2,1)} reshape(bf16[32,1,192,512]{3,2,1,0:T(8,128)(2,1)} %get-tuple-element.10) | data formatting | bytes 12582912 | tf_op jit(solution)/shard_map/reshape;squeeze | solution.py:314
  52.9 4.6 %fusion.16 = f32[32,4,4,128]{3,2,1,0:T(4,128)S(1)} fusion(bf16[32,192,4,128]{3,2,1,0:T(4,128)(2,1)} %reshape_squeeze.12, f32[32,4,4,192]{3,2,1,0:T(4,128)S(1)} %get-tuple-element.27, f32[32,4,4]{2,1,0:T(4,128)S(1)} %get-tuple-element.21, f32[32,4,4]{2,1,0:T(4,128)S(1)} %multiply_maximum_fusion, f32[32,4,128]{2,1,0:T(4,128)S(1)} %bitcast.75, ...), kind=kOutput, calls=%fused_computation.14 | convolution fusion | flops 25722880 | bytes 7018496 | tf_op jit(solution)/shard_map/skgl,slkd->skgd/dot_general | solution.py:340
  57.5 0.1 reshape.154
  57.7 0.1 eq.50
  57.9 0.1 and.66
  58.2 0.2 select_reduce_fusion
  58.4 0.1 reduce_sum.32
  58.6 0.1 multiply_reduce_fusion
  58.8 0.2 fusion.29
  59.0 4.5 %all-reduce = (f32[32]{0:T(128)S(1)}, f32[32,8]{0,1:T(8,128)S(1)}) all-reduce(f32[32]{0:T(128)S(1)} %multiply_reduce_fusion, f32[32,8]{0,1:T(8,128)S(1)} %fusion.29), channel_id=1, replica_groups=mesh['grp'=8,'ep'=8,'tp'=2] {'tp'}, use_global_device_ids=true, to_apply=%region_4.5 | all-reduce | flops 288 | bytes 2304 | tf_op jit(solution)/shard_map/psum | solution.py:378
  63.6 3.6 %dynamic-slice_bitcast_fusion = (bf16[256,2048]{1,0:T(8,128)(2,1)}, bf16[256,2048]{1,0:T(8,128)(2,1)}, bf16[256,2048]{1,0:T(8,128)(2,1)}) fusion(bf16[1,256,8192]{2,1,0:T(8,128)(2,1)} %param.23, s32[]{:T(128)S(6)} %select_n.58, s32[]{:T(128)S(6)} %select_n.56, s32[]{:T(128)S(6)} %select_n.57), kind=kLoop, calls=%fused_computation.16 | loop fusion | bytes 6291468 | tf_op jit(solution)/shard_map/dynamic_slice | solution.py:373
  67.3 1.8 collective-permute-start.5
  69.1 2.0 collective-permute-start.7
  71.1 1.6 collective-permute-start.8
  72.7 33.8 %all_gather.3 = bf16[32,4096]{1,0:T(8,128)(2,1)S(1)} all-gather(bf16[32,2048]{1,0:T(8,128)(2,1)S(1)} %divide_convert_fusion.2), channel_id=1, replica_groups=mesh['grp'=8,'ep'=8,'tp'=2] {'tp'}, dimensions={1}, use_global_device_ids=true | all-gather | bytes 393216 | tf_op jit(solution)/shard_map/all_gather | solution.py:387
  106.7 0.3 fusion.4
  107.0 1.1 copy.64
  108.1 4.6 %all-to-all-start = ((bf16[8,8,4096]{2,0,1:T(8,128)(2,1)}), bf16[8,8,4096]{2,0,1:T(8,128)(2,1)S(1)}, u32[]{:S(2)}, u32[]{:S(2)}) async-start(bf16[8,8,4096]{2,0,1:T(8,128)(2,1)} %copy.64), calls=%async_computation | async-start | bytes 1048576 | tf_op jit(solution)/shard_map/all_to_all | solution.py:420
  112.8 0.1 copy.56
  113.0 0.1 reshape.155
  113.2 8.8 %all-to-all-done = bf16[8,8,4096]{2,0,1:T(8,128)(2,1)S(1)} async-done(((bf16[8,8,4096]{2,0,1:T(8,128)(2,1)}), bf16[8,8,4096]{2,0,1:T(8,128)(2,1)S(1)}, u32[]{:S(2)}, u32[]{:S(2)}) %all-to-all-start) | async-done | bytes 524320 | tf_op jit(solution)/shard_map/all_to_all | solution.py:420
  122.0 0.8 copy-done.4
  122.8 104.7 %expert_layer.1 = bf16[64,4096]{1,0:T(8,128)(2,1)} custom-call(bf16[64,4096]{1,0:T(8,128)(2,1)} %bitcast.71, bf16[256,8192]{1,0:T(8,128)(2,1)} %bitcast.68, bf16[256,8192]{1,0:T(8,128)(2,1)} %bitcast.69, bf16[256,8192]{1,0:T(8,128)(2,1)} %bitcast.70, bf16[256,2048]{1,0:T(8,128)(2,1)} %collective-permute-done.g1, ...), custom_call_target="tpu_custom_call" | custom-call | flops 12999999488 | bytes 14000000 | tf_op jit(solution)/shard_map/expert_layer/pallas_call | solution.py:292
  227.5 0.5 broadcast.146
  228.0 2.0 reduce.4
  230.1 1.3 reshape.171
  231.4 8.3 %all-to-all-start.1 = ((bf16[8,2,16384]{2,1,0:T(2,128)(2,1)}), bf16[8,2,16384]{2,1,0:T(2,128)(2,1)S(1)}, u32[]{:S(2)}, u32[]{:S(2)}) async-start(bf16[8,2,16384]{2,1,0:T(2,128)(2,1)} %reshape.171), calls=%async_computation.1 | async-start | bytes 1048576 | tf_op jit(solution)/shard_map/all_to_all | solution.py:423
  239.7 0.7 gather_fusion
  240.6 0.2 subtract_reduce_fusion
  240.8 8.3 %all-to-all-done.1 = bf16[8,2,16384]{2,1,0:T(2,128)(2,1)S(1)} async-done(((bf16[8,2,16384]{2,1,0:T(2,128)(2,1)}), bf16[8,2,16384]{2,1,0:T(2,128)(2,1)S(1)}, u32[]{:S(2)}, u32[]{:S(2)}) %all-to-all-start.1) | async-done | bytes 524320 | tf_op jit(solution)/shard_map/all_to_all | solution.py:423
  249.1 0.5 reshape.172
  249.6 0.6 copy.114
  250.2 0.4 convolution_multiply_fusion.1
  250.7 1.1 fusion.6
  251.8 11.8 %reduce-scatter.2.cloned.1.call-done = bf16[32,2048]{1,0:T(8,128)(2,1)} async-done(((bf16[32,4096]{1,0:T(8,128)(2,1)}), bf16[32,2048]{1,0:T(8,128)(2,1)}) %reduce-scatter.2.cloned.1.call-update) | async-done | bytes 131088 | tf_op jit(solution)/shard_map/reduce_scatter | solution.py:429
  263.6 1.6 select_convert_fusion
  (61 shorter events, 1.6 us)
Async XLA Ops:
  6.5 52.3 %copy-start = (bf16[2048,8]{0,1:T(8,128)(2,1)S(1)}, bf16[2048,8]{0,1:T(8,128)(2,1)}, u32[]{:S(2)}) copy-start(bf16[2048,8]{0,1:T(8,128)(2,1)} %param.20) | copy-start | bytes 98308
  6.5 14.6 %copy-start.2 = (bf16[32,2,192,512]{3,2,1,0:T(8,128)(2,1)S(1)}, bf16[32,2,192,512]{3,2,1,0:T(8,128)(2,1)}, u32[]{:S(2)}) copy-start(bf16[32,2,192,512]{3,2,1,0:T(8,128)(2,1)} %param.15) | copy-start | bytes 37748740
  10.4 56.9 %collective-permute-start = (bf16[256,2048]{1,0:T(8,128)(2,1)}, bf16[256,2048]{1,0:T(8,128)(2,1)}, u32[]{:S(2)}, u32[]{:S(2)}) collective-permute-start(bf16[256,2048]{1,0:T(8,128)(2,1)} %get-tuple-element.18), channel_id=1, source_target_pairs={{0,16},{1,17},{2,3},{3,66},{4,20},{5,21},{6,7},{7,70},{8,24},{9,25... | collective-permute-start | bytes 3145736 | tf_op jit(solution)/shard_map/ppermute | solution.py:374
  12.8 56.3 %collective-permute-start.1 = (bf16[256,2048]{1,0:T(8,128)(2,1)}, bf16[256,2048]{1,0:T(8,128)(2,1)}, u32[]{:S(2)}, u32[]{:S(2)}) collective-permute-start(bf16[256,2048]{1,0:T(8,128)(2,1)} %get-tuple-element.19), channel_id=1, source_target_pairs={{0,32},{1,33},{2,66},{3,67},{4,36},{5,37},{6,70},{7,71},{8,40},{9,... | collective-permute-start | bytes 3145736 | tf_op jit(solution)/shard_map/ppermute | solution.py:374
  16.1 53.0 %collective-permute-start.2 = (bf16[256,2048]{1,0:T(8,128)(2,1)}, bf16[256,2048]{1,0:T(8,128)(2,1)}, u32[]{:S(2)}, u32[]{:S(2)}) collective-permute-start(bf16[256,2048]{1,0:T(8,128)(2,1)} %get-tuple-element.17), channel_id=1, source_target_pairs={{0,48},{1,49},{2,67},{3,2},{4,52},{5,53},{6,71},{7,6},{8,56},{9,57... | collective-permute-start | bytes 3145736 | tf_op jit(solution)/shard_map/ppermute | solution.py:374
  20.0 51.2 %collective-permute-start.3 = (bf16[256,2048]{1,0:T(8,128)(2,1)}, bf16[256,2048]{1,0:T(8,128)(2,1)}, u32[]{:S(2)}, u32[]{:S(2)}) collective-permute-start(bf16[256,2048]{1,0:T(8,128)(2,1)} %get-tuple-element.15), channel_id=1, source_target_pairs={{0,16},{1,17},{2,3},{3,66},{4,20},{5,21},{6,7},{7,70},{8,24},{9,25... | collective-permute-start | bytes 3145736 | tf_op jit(solution)/shard_map/ppermute | solution.py:374
  20.7 101.3 %collective-permute-start.4 = (bf16[256,2048]{1,0:T(8,128)(2,1)S(1)}, bf16[256,2048]{1,0:T(8,128)(2,1)}, u32[]{:S(2)}, u32[]{:S(2)}) collective-permute-start(bf16[256,2048]{1,0:T(8,128)(2,1)S(1)} %get-tuple-element.16), channel_id=1, source_target_pairs={{0,32},{1,33},{2,66},{3,67},{4,36},{5,37},{6,70},{7,71},{8,40},{9,... | collective-permute-start | bytes 3145736 | tf_op jit(solution)/shard_map/ppermute | solution.py:374
  26.0 9.7 %copy-start.5 = (bf16[32,2048]{1,0:T(8,128)(2,1)S(1)}, bf16[32,2048]{1,0:T(8,128)(2,1)}, u32[]{:S(2)}) copy-start(bf16[32,2048]{1,0:T(8,128)(2,1)} %param.13) | copy-start | bytes 393220
  26.0 9.8 %copy-start.9 = (s32[32]{0:T(128)S(1)}, s32[32]{0:T(128)}, u32[]{:S(2)}) copy-start(s32[32]{0:T(128)} %param.16) | copy-start | bytes 388
  26.0 9.9 %copy-start.6 = (bf16[32,2,512]{2,1,0:T(2,128)(2,1)S(1)}, bf16[32,2,512]{2,1,0:T(2,128)(2,1)}, u32[]{:S(2)}) copy-start(bf16[32,2,512]{2,1,0:T(2,128)(2,1)} %param.14) | copy-start | bytes 196612
  52.8 4.8 %copy-start.7 = (bf16[2048]{0:T(1024)(128)(2,1)S(1)}, bf16[2048]{0:T(1024)(128)(2,1)}, u32[]{:S(2)}) copy-start(bf16[2048]{0:T(1024)(128)(2,1)} %param.19) | copy-start | bytes 12292
  52.8 4.8 %copy-start.8 = (s32[32,2]{0,1:T(2,128)S(1)}, s32[32,2]{0,1:T(2,128)}, u32[]{:S(2)}) copy-start(s32[32,2]{0,1:T(2,128)} %param.18) | copy-start | bytes 772
  52.9 5.0 %copy-start.10 = (s32[32]{0:T(128)S(1)}, s32[32]{0:T(128)}, u32[]{:S(2)}) copy-start(s32[32]{0:T(128)} %param.17) | copy-start | bytes 388
  52.9 5.8 %copy-start.3 = (bf16[32,2048]{1,0:T(8,128)(2,1)S(1)}, bf16[32,2048]{1,0:T(8,128)(2,1)}, u32[]{:S(2)}) copy-start(bf16[32,2048]{1,0:T(8,128)(2,1)} %param.12) | copy-start | bytes 393220
  67.3 54.7 %collective-permute-start.5 = (bf16[256,2048]{1,0:T(8,128)(2,1)S(1)}, bf16[256,2048]{1,0:T(8,128)(2,1)}, u32[]{:S(2)}, u32[]{:S(2)}) collective-permute-start(bf16[256,2048]{1,0:T(8,128)(2,1)S(1)} %get-tuple-element.14), channel_id=1, source_target_pairs={{0,48},{1,49},{2,67},{3,2},{4,52},{5,53},{6,71},{7,6},{8,56},{9,57... | collective-permute-start | bytes 3145736 | tf_op jit(solution)/shard_map/ppermute | solution.py:374
  69.1 52.9 %collective-permute-start.6 = (bf16[256,2048]{1,0:T(8,128)(2,1)}, bf16[256,2048]{1,0:T(8,128)(2,1)}, u32[]{:S(2)}, u32[]{:S(2)}) collective-permute-start(bf16[256,2048]{1,0:T(8,128)(2,1)} %get-tuple-element.12), channel_id=1, source_target_pairs={{0,16},{1,17},{2,3},{3,66},{4,20},{5,21},{6,7},{7,70},{8,24},{9,25... | collective-permute-start | bytes 3145736 | tf_op jit(solution)/shard_map/ppermute | solution.py:374
  69.1 52.9 %collective-permute-start.7 = (bf16[256,2048]{1,0:T(8,128)(2,1)}, bf16[256,2048]{1,0:T(8,128)(2,1)}, u32[]{:S(2)}, u32[]{:S(2)}) collective-permute-start(bf16[256,2048]{1,0:T(8,128)(2,1)} %get-tuple-element.13), channel_id=1, source_target_pairs={{0,32},{1,33},{2,66},{3,67},{4,36},{5,37},{6,70},{7,71},{8,40},{9,... | collective-permute-start | bytes 3145736 | tf_op jit(solution)/shard_map/ppermute | solution.py:374
  71.1 50.9 %collective-permute-start.8 = (bf16[256,2048]{1,0:T(8,128)(2,1)}, bf16[256,2048]{1,0:T(8,128)(2,1)}, u32[]{:S(2)}, u32[]{:S(2)}) collective-permute-start(bf16[256,2048]{1,0:T(8,128)(2,1)} %get-tuple-element.11), channel_id=1, source_target_pairs={{0,48},{1,49},{2,67},{3,2},{4,52},{5,53},{6,71},{7,6},{8,56},{9,57... | collective-permute-start | bytes 3145736 | tf_op jit(solution)/shard_map/ppermute | solution.py:374
  108.1 13.9 %all-to-all-start = ((bf16[8,8,4096]{2,0,1:T(8,128)(2,1)}), bf16[8,8,4096]{2,0,1:T(8,128)(2,1)S(1)}, u32[]{:S(2)}, u32[]{:S(2)}) async-start(bf16[8,8,4096]{2,0,1:T(8,128)(2,1)} %copy.64), calls=%async_computation | async-start | bytes 1048576 | tf_op jit(solution)/shard_map/all_to_all | solution.py:420
  122.0 0.8 copy-start.4
  231.4 17.7 %all-to-all-start.1 = ((bf16[8,2,16384]{2,1,0:T(2,128)(2,1)}), bf16[8,2,16384]{2,1,0:T(2,128)(2,1)S(1)}, u32[]{:S(2)}, u32[]{:S(2)}) async-start(bf16[8,2,16384]{2,1,0:T(2,128)(2,1)} %reshape.171), calls=%async_computation.1 | async-start | bytes 1048576 | tf_op jit(solution)/shard_map/all_to_all | solution.py:423
  239.7 23.9 %reduce-scatter.2.cloned.1.call-start = ((), (), s32[]{:S(2)}) async-start(), calls=%async_computation.3 | async-start | bytes 393216 | tf_op jit(solution)/shard_map/reduce_scatter | solution.py:429
  239.7 25.5 %copy-start.1 = (bf16[2048,8]{0,1:T(8,128)(2,1)S(1)}, bf16[2048,8]{0,1:T(8,128)(2,1)}, u32[]{:S(2)}) copy-start(bf16[2048,8]{0,1:T(8,128)(2,1)} %param.20) | copy-start | bytes 98308
Sparse Core Ops, SparseCore 0:
  252.0 11.5 reduce-scatter.1
